TPU v7x, 32 devices: a whole 2x2x4 slice. The times are simulated.
32 devices in a mesh: group: 2 (over y), phi: 4 (over z), eta: 2 (over x), half: 2 (over core).
Axes of the slice: x: 2, y: 2, z: 4, core: 2. Of those that a mesh axis runs over, the one named last changes fastest.
Arguments:
- feats: bfloat16 [8, 2, 512, 512], P(('group', 'phi'), 'eta', 'half'), parts along dimension 0, may hold values from -6 to 6
- cotangent: bfloat16 [8, 2, 512, 512], P(('group', 'phi'), 'eta', 'half'), parts along dimension 0, may hold values from -6 to 6
- tiles: bfloat16 [8, 2, 24, 128, 128], P(('group', 'phi'), 'eta', 'half'), parts along dimension 0, may hold values from -0.21875 to 0.21875
- tile_src: int32 [8, 2, 24], P(('group', 'phi'), 'eta', 'half'), parts along dimension 0, may hold values from 0 to 5
- tile_dst: int32 [8, 2, 24], P(('group', 'phi'), 'eta', 'half'), parts along dimension 0, may hold values from -1 to 3, as said below
- weights: bfloat16 [2, 512, 512], replicated, may hold values from -0.25 to 0.25
- mask: int32 [2, 8, 8], replicated, may hold values 0 or 1
- counts: int32 [8, 2], P(('group', 'phi'), 'eta'), parts along dimension 0, may hold values from 128 to 512, as said below
Outputs:
- final: bfloat16 [8, 2, 512, 512], P(('group', 'phi'), 'eta', 'half'), parts along dimension 0
- grad_w: float32 [4, 512, 512], P('group', 'phi'), parts along dimension 0
There are 2 independent parts, one for each index of `group`. A program takes and returns all parts, laid end to end along the dimension named above; an argument that names none is the same for every part. Nothing has to cross between parts.
Inputs may be any that keep to these rules, and one draw needn't show every extreme that they name: `tile_dst`: in each region half the live tiles fill the first slots and the rest hold -1; some region half has all 12 slots live. `counts`: some region is full and some holds a quarter of its hits.
All inputs are finite; a program needn't handle non-finite values.
Results may differ from a plain program's by a relative error of at most 0.017.
Values may be sent and summed in bfloat16 or wider, within the bound.
No kernel may reach another device: no remote copies, remote signals or barrier semaphores. Data moves between devices by JAX's collectives and lax.ppermute only.
A program may use at most 64 MiB of HBM per device.

v0:
```python
import jax
import jax.numpy as jnp
from jax import lax
from jax.sharding import PartitionSpec as P


def with_halo(block, sides, width, periodic):
    for axis, dim in sides:
        count = lax.axis_size(axis)
        forward = [(i, i + 1) for i in range(count - 1)]
        if periodic:
            forward.append((count - 1, 0))
        backward = [(target, source) for source, target in forward]
        low = lax.ppermute(
            lax.slice_in_dim(block, block.shape[dim] - width, None, axis=dim), axis, forward
        )
        high = lax.ppermute(lax.slice_in_dim(block, 0, width, axis=dim), axis, backward)
        block = jnp.concatenate([low, block, high], axis=dim)
    return block


def silu_slope(pre):
    sigma = jax.nn.sigmoid(pre)
    return sigma * (1.0 + pre * (1.0 - sigma))


def body(feats, cotangent, tiles, tile_src, tile_dst, weights, mask, counts):
    rows = feats.shape[2]
    width = feats.shape[3]
    block = tiles.shape[3]
    own_blocks = rows // block
    halves = lax.axis_size("half")
    region_blocks = own_blocks * halves
    slots = own_blocks + 4
    layers = weights.shape[0]
    grid = mask.shape[1]
    side = width // grid
    tile_set = tiles[0, 0]
    sources_of = tile_src[0, 0]
    targets = tile_dst[0, 0]
    first_row = lax.axis_index("half") * rows
    live = (first_row + jnp.arange(rows, dtype=jnp.int32) < counts[0, 0]).astype(jnp.float32)[
        :, None
    ]
    eta_here = lax.axis_index("eta")
    lower_eta = (eta_here > 0).astype(jnp.bfloat16)
    upper_eta = (eta_here < lax.axis_size("eta") - 1).astype(jnp.bfloat16)
    mask_full = (
        jnp.broadcast_to(mask[:, :, None, :, None], (layers, grid, side, grid, side))
        .reshape(layers, width, width)
        .astype(jnp.float32)
    )
    masked = (weights.astype(jnp.float32) * mask_full).astype(jnp.bfloat16)
    block_ids = jnp.arange(region_blocks, dtype=jnp.int32)
    slot_ids = jnp.arange(slots, dtype=jnp.int32)
    state = feats[0, 0]
    inputs = []
    pres = []
    for layer in range(layers):
        edge = state[:block][None, None]
        padded = with_halo(edge, (("phi", 0), ("eta", 1)), 1, True)
        rims = jnp.stack(
            [padded[0, 1], padded[2, 1], padded[1, 0] * lower_eta, padded[1, 2] * upper_eta]
        )
        messages_picked = jnp.take(
            jnp.concatenate([state.reshape(own_blocks, block, width), rims], axis=0),
            sources_of,
            axis=0,
        )
        messages_parts = jnp.einsum(
            "tij,tjd->tid", tile_set, messages_picked, preferred_element_type=jnp.float32
        )
        messages_onehot = (targets[None, :] == block_ids[:, None]).astype(jnp.float32)
        messages_total = jnp.einsum(
            "bt,tid->bid", messages_onehot, messages_parts, precision=lax.Precision.HIGHEST
        )
        region = messages_total.reshape(region_blocks * block, width)
        gathered = lax.psum_scatter(
            region.astype(jnp.bfloat16), "half", scatter_dimension=0, tiled=True
        ).astype(jnp.float32)
        hfloat = state.astype(jnp.float32)
        mixed = (hfloat + gathered).astype(jnp.bfloat16)
        pre = jnp.dot(mixed, masked[layer], preferred_element_type=jnp.float32)
        state = (live * (hfloat + jax.nn.silu(pre))).astype(jnp.bfloat16)
        inputs.append(mixed)
        pres.append(pre)
    upstream = cotangent[0, 0].astype(jnp.float32)
    partials = [None] * layers
    for layer in reversed(range(layers)):
        delta = (upstream * live * silu_slope(pres[layer])).astype(jnp.bfloat16)
        partials[layer] = (
            jnp.einsum("rd,re->de", inputs[layer], delta, preferred_element_type=jnp.float32)
            * mask_full[layer]
        )
        if layer > 0:
            back = jnp.einsum(
                "re,de->rd", delta, masked[layer], preferred_element_type=jnp.float32
            ).astype(jnp.bfloat16)
            whole = lax.all_gather(back, "half", axis=0, tiled=True)
            valid = (targets >= 0).astype(jnp.bfloat16)
            picked = (
                jnp.take(
                    whole.reshape(region_blocks, block, width), jnp.maximum(targets, 0), axis=0
                )
                * valid[:, None, None]
            )
            parts = jnp.einsum("tji,tjd->tid", tile_set, picked, preferred_element_type=jnp.float32)
            onehot = (sources_of[None, :] == slot_ids[:, None]).astype(jnp.float32)
            total = jnp.einsum("st,tid->sid", onehot, parts, precision=lax.Precision.HIGHEST)
            returned_phi = with_halo(
                total[own_blocks : own_blocks + 2].astype(jnp.bfloat16), (("phi", 0),), 1, True
            ).astype(jnp.float32)
            returned_eta = with_halo(
                total[own_blocks + 2 :].astype(jnp.bfloat16), (("eta", 0),), 1, False
            ).astype(jnp.float32)
            extra = returned_phi[0] + returned_phi[3] + returned_eta[0] + returned_eta[3]
            own = total[:own_blocks].reshape(rows, width)
            own = jnp.concatenate([own[:block] + extra, own[block:]], axis=0)
            upstream = live * upstream + back.astype(jnp.float32) + own
    stacked = jnp.stack(partials)
    shares = lax.psum_scatter(stacked.astype(jnp.bfloat16), "phi", scatter_dimension=1, tiled=True)
    result = lax.psum(shares, ("eta", "half")).astype(jnp.float32)
    return (state[None, None], result)


def solution(mesh):
    in_specs = (
        P(("group", "phi"), "eta", "half", None),
        P(("group", "phi"), "eta", "half", None),
        P(("group", "phi"), "eta", "half", None, None),
        P(("group", "phi"), "eta", "half"),
        P(("group", "phi"), "eta", "half"),
        P(),
        P(),
        P(("group", "phi"), "eta"),
    )
    out_specs = (P(("group", "phi"), "eta", "half", None), P("group", "phi", None))
    return jax.shard_map(body, mesh=mesh, in_specs=in_specs, out_specs=out_specs, check_vma=False)
```

profile of v0, /device:TPU:0, one launch (start us, length us, event | category | flops | bytes accessed | tf_op | source)
XLA Modules:
  0.0 213.0 jit_solution(10340029275667400948)
XLA Ops:
  7.2 1.0 slice.89
  8.2 3.1 %collective-permute-start = (bf16[1,1,128,512]{3,2,1,0:T(8,128)(2,1)S(1)}, bf16[1,1,128,512]{3,2,1,0:T(8,128)(2,1)S(1)}, u32[]{:S(2)}, u32[]{:S(2)}) collective-permute-start(bf16[1,1,128,512]{3,2,1,0:T(8,128)(2,1)S(1)} %slice.89), channel_id=1, source_target_pairs={{0,4},{4,8},{8,12},{12,0},{1,5},{5,9},{9,13},{13,1},{2,6},{6,10},{... | collective-permute-start | bytes 393224 | tf_op jit(solution)/shard_map/ppermute | solution.py:14
  11.3 2.1 collective-permute-start.1
  13.4 0.7 compare_select_fusion
  14.0 0.7 compare_and_fusion
  14.7 1.0 constant_dynamic-update-slice_fusion
  15.7 1.9 collective-permute-done
  17.6 1.4 collective-permute-done.1
  19.1 1.6 collective-permute-start.2
  20.6 0.5 collective-permute-start.3
  21.2 10.0 %collective-permute-done.2 = bf16[3,1,128,512]{3,2,1,0:T(8,128)(2,1)S(1)} collective-permute-done((bf16[3,1,128,512]{3,2,1,0:T(8,128)(2,1)S(1)}, bf16[3,1,128,512]{3,2,1,0:T(8,128)(2,1)S(1)}, u32[]{:S(2)}, u32[]{:S(2)}) %collective-permute-start.2) | collective-permute-done | bytes 393248 | tf_op jit(solution)/shard_map/ppermute | solution.py:14
  31.2 6.8 %collective-permute-done.3 = bf16[3,1,128,512]{3,2,1,0:T(8,128)(2,1)S(1)} collective-permute-done((bf16[3,1,128,512]{3,2,1,0:T(8,128)(2,1)S(1)}, bf16[3,1,128,512]{3,2,1,0:T(8,128)(2,1)S(1)}, u32[]{:S(2)}, u32[]{:S(2)}) %collective-permute-start.3) | collective-permute-done | bytes 393248 | tf_op jit(solution)/shard_map/ppermute | solution.py:17
  38.0 1.9 gather_fusion.1
  39.9 2.1 fusion.8
  42.0 3.5 %copy.19 = f32[12,512,128]{1,0,2:T(8,128)} copy(f32[12,512,128]{2,1,0:T(8,128)S(1)} %fusion.8) | data formatting | bytes 6291456 | tf_op jit(solution)/shard_map/tij,tjd->tid/dot_general | solution.py:70
  45.5 3.8 %fusion.16 = bf16[4,128,512]{2,0,1:T(4,128)(2,1)S(1)} fusion(f32[12,512,128]{1,0,2:T(8,128)} %copy.19, s32[12]{0:T(128)S(1)} %bitcast.122), kind=kOutput, calls=%fused_computation.22 | convolution fusion | flops 38010928 | bytes 3670064 | tf_op jit(solution)/shard_map/bt,tid->bid/dot_general | solution.py:74
  49.3 0.9 copy.14
  50.3 2.3 %broadcast_in_dim.41 = f32[2,8,64,8,64]{4,3,2,1,0:T(8,128)} broadcast(f32[2,8,8]{2,1,0:T(8,128)S(1)} %convert_element_type.115), dimensions={0,1,3} | broadcast | bytes 2097664 | tf_op jit(solution)/shard_map/broadcast_in_dim | solution.py:49
  52.6 3.5 %convert_element_type.116 = f32[2,512,512]{2,1,0:T(8,128)S(1)} reshape(f32[2,8,64,8,64]{4,3,2,1,0:T(8,128)} %broadcast_in_dim.41) | data formatting | bytes 4194304 | tf_op jit(solution)/shard_map/convert_element_type | solution.py:51
  56.8 0.6 compare_convert_fusion.1
  57.3 1.3 multiply_convert_fusion
  58.7 2.4 %fusion.35 = (bf16[256,512]{1,0:T(8,128)(2,1)S(1)}, f32[256,512]{1,0:T(8,128)}) fusion(bf16[1,1,256,512]{3,2,1,0:T(8,128)(2,1)} %param.10, f32[256]{0:T(256)} %compare_convert_fusion.1, bf16[2,512,512]{2,1,0:T(8,128)(2,1)} %multiply_convert_fusion, bf16[256,512]{1,0:T(8,128)(2,1)} %reduce-scatter.4.cloned.1.call-done), kind=kOutput, calls=%fused_computation.43 | convolution fusion | flops 135790592 | bytes 2098176 | tf_op jit(solution)/shard_map/dot_general | solution.py:83
  61.1 1.8 collective-permute-start.4
  62.9 2.1 collective-permute-start.5
  65.0 4.4 %collective-permute-done.4 = bf16[1,1,128,512]{3,2,1,0:T(8,128)(2,1)S(1)} collective-permute-done((bf16[1,1,128,512]{3,2,1,0:T(8,128)(2,1)S(1)}, bf16[1,1,128,512]{3,2,1,0:T(8,128)(2,1)S(1)}, u32[]{:S(2)}, u32[]{:S(2)}) %collective-permute-start.4) | collective-permute-done | bytes 131104 | tf_op jit(solution)/shard_map/ppermute | solution.py:14
  69.4 1.1 collective-permute-done.5
  70.5 1.5 collective-permute-start.6
  72.0 0.6 collective-permute-start.7
  72.6 10.0 %collective-permute-done.6 = bf16[3,1,128,512]{3,2,1,0:T(8,128)(2,1)S(1)} collective-permute-done((bf16[3,1,128,512]{3,2,1,0:T(8,128)(2,1)S(1)}, bf16[3,1,128,512]{3,2,1,0:T(8,128)(2,1)S(1)}, u32[]{:S(2)}, u32[]{:S(2)}) %collective-permute-start.6) | collective-permute-done | bytes 393248 | tf_op jit(solution)/shard_map/ppermute | solution.py:14
  82.7 6.9 %collective-permute-done.7 = bf16[3,1,128,512]{3,2,1,0:T(8,128)(2,1)S(1)} collective-permute-done((bf16[3,1,128,512]{3,2,1,0:T(8,128)(2,1)S(1)}, bf16[3,1,128,512]{3,2,1,0:T(8,128)(2,1)S(1)}, u32[]{:S(2)}, u32[]{:S(2)}) %collective-permute-start.7) | collective-permute-done | bytes 393248 | tf_op jit(solution)/shard_map/ppermute | solution.py:17
  89.6 1.9 gather_fusion.2
  91.5 2.1 fusion.6
  93.6 3.5 %copy.20 = f32[12,512,128]{1,0,2:T(8,128)} copy(f32[12,512,128]{2,1,0:T(8,128)S(1)} %fusion.6) | data formatting | bytes 6291456 | tf_op jit(solution)/shard_map/tij,tjd->tid/dot_general | solution.py:70
  97.1 3.8 %fusion.19 = bf16[4,128,512]{2,0,1:T(4,128)(2,1)S(1)} fusion(f32[12,512,128]{1,0,2:T(8,128)} %copy.20, s32[12]{0:T(128)S(1)} %bitcast.123), kind=kOutput, calls=%fused_computation.23 | convolution fusion | flops 38010928 | bytes 3670064 | tf_op jit(solution)/shard_map/bt,tid->bid/dot_general | solution.py:74
  100.9 0.9 copy.15
  101.8 0.0 reduce-scatter.8.cloned.1.call-start
  101.8 0.2 broadcast_in_dim.46
  102.0 1.5 squeeze.38
  103.5 0.2 broadcast_in_dim.47
  103.8 1.5 squeeze.39
  105.3 4.0 %reduce-scatter.6.cloned.1.call-done = bf16[256,512]{1,0:T(8,128)(2,1)} async-done(((bf16[512,512]{1,0:T(8,128)(2,1)}), bf16[256,512]{1,0:T(8,128)(2,1)}) %reduce-scatter.6.cloned.1.call-update) | async-done | bytes 262160 | tf_op jit(solution)/shard_map/reduce_scatter | solution.py:78
  109.3 2.4 %fusion.42 = (bf16[256,512]{1,0:T(8,128)(2,1)S(1)}, bf16[1,1,256,512]{3,2,1,0:T(8,128)(2,1)}) fusion(bf16[1,1,256,512]{3,2,1,0:T(8,128)(2,1)S(1)} %copy-done.19, f32[256]{0:T(256)S(1)} %copy-done.17, bf16[256,512]{1,0:T(8,128)(2,1)S(1)} %copy-done.3, bf16[2,512,512]{2,1,0:T(8,128)(2,1)} %multiply_convert_fusion, ...), kind=kOutput, calls=%fused_computation.54 | convolution fusion | flops 136839168 | bytes 2098176 | tf_op jit(solution)/shard_map/dot_general | solution.py:83
  111.7 0.3 convolution_convert_fusion
  112.0 0.7 copy-done.9
  112.7 2.3 %all_gather.3 = bf16[512,512]{1,0:T(8,128)(2,1)S(1)} all-gather(bf16[256,512]{1,0:T(8,128)(2,1)S(1)} %convolution_convert_fusion), channel_id=1, replica_groups=mesh['group'=2,'phi'=4,'eta'=2,'half'=2] {'half'}, dimensions={0}, use_global_device_ids=true | all-gather | bytes 786432 | tf_op jit(solution)/shard_map/all_gather | solution.py:99
  115.1 1.9 gather_fusion
  116.9 2.1 %fusion.10 = f32[12,512,128]{2,1,0:T(8,128)S(1)} fusion(bf16[12,128,512]{2,1,0:T(8,128)(2,1)} %gather_fusion, pred[12]{0:T(512)(128)(4,1)S(1)} %get-tuple-element.18, bf16[12]{0:T(256)(128)(2,1)S(1)} %get-tuple-element.17, bf16[1,1,12,128,128]{4,3,2,1,0:T(8,128)(2,1)S(1)} %copy-done), kind=kOutput, calls=%fused_computation.14 | convolution fusion | flops 202899456 | bytes 5111844 | tf_op jit(solution)/shard_map/tji,tjd->tid/dot_general | solution.py:107
  119.1 3.5 %copy.21 = f32[12,512,128]{1,0,2:T(8,128)} copy(f32[12,512,128]{2,1,0:T(8,128)S(1)} %fusion.10) | data formatting | bytes 6291456 | tf_op jit(solution)/shard_map/tji,tjd->tid/dot_general | solution.py:107
  122.6 3.7 %fusion = f32[6,128,512]{2,0,1:T(8,128)S(1)} fusion(f32[12,512,128]{1,0,2:T(8,128)} %copy.21, s32[12]{0:T(128)S(1)} %bitcast.124), kind=kOutput, calls=%fused_computation.3 | convolution fusion | flops 56623176 | bytes 4718640 | tf_op jit(solution)/shard_map/st,tid->sid/dot_general | solution.py:109
  126.3 0.9 fusion.80
  127.4 3.8 %collective-permute-start.10 = (bf16[1,128,512]{2,1,0:T(8,128)(2,1)S(1)}, bf16[1,128,512]{2,1,0:T(8,128)(2,1)S(1)}, u32[]{:S(2)}, u32[]{:S(2)}) collective-permute-start(bf16[1,128,512]{2,1,0:T(8,128)(2,1)S(1)} %get-tuple-element.9), channel_id=1, source_target_pairs={{0,2},{1,3},{4,6},{5,7},{8,10},{9,11},{12,14},{13,15},{16,18},{17,... | collective-permute-start | bytes 393224 | tf_op jit(solution)/shard_map/ppermute | solution.py:14
  131.1 1.3 collective-permute-start.11
  132.4 1.5 collective-permute-start.8
  134.0 2.3 %collective-permute-start.9 = (bf16[1,128,512]{2,1,0:T(8,128)(2,1)S(1)}, bf16[1,128,512]{2,1,0:T(8,128)(2,1)S(1)}, u32[]{:S(2)}, u32[]{:S(2)}) collective-permute-start(bf16[1,128,512]{2,1,0:T(8,128)(2,1)S(1)} %get-tuple-element.10), channel_id=1, source_target_pairs={{4,0},{8,4},{12,8},{0,12},{5,1},{9,5},{13,9},{1,13},{6,2},{10,6},{... | collective-permute-start | bytes 393224 | tf_op jit(solution)/shard_map/ppermute | solution.py:17
  136.3 0.3 fusion.24
  136.7 1.7 collective-permute-done.11
  138.5 2.2 %collective-permute-done.8 = bf16[1,128,512]{2,1,0:T(8,128)(2,1)S(1)} collective-permute-done((bf16[1,128,512]{2,1,0:T(8,128)(2,1)S(1)}, bf16[1,128,512]{2,1,0:T(8,128)(2,1)S(1)}, u32[]{:S(2)}, u32[]{:S(2)}) %collective-permute-start.8) | collective-permute-done | bytes 131104 | tf_op jit(solution)/shard_map/ppermute | solution.py:14
  140.7 1.3 collective-permute-done.9
  141.9 0.1 fusion.50
  142.1 0.6 fusion.25
  142.7 1.1 pad_maximum_fusion
  143.9 27.9 %reduce-scatter.8.cloned.1.call-done = bf16[2,128,512]{2,1,0:T(8,128)(2,1)} async-done(((bf16[2,512,512]{2,1,0:T(8,128)(2,1)}), bf16[2,128,512]{2,1,0:T(8,128)(2,1)}) %reduce-scatter.8.cloned.1.call-update) | async-done | bytes 262160 | tf_op jit(solution)/shard_map/reduce_scatter | solution.py:121
  171.8 32.9 %all-reduce.2.cloned.1.call-done = bf16[2,128,512]{2,1,0:T(8,128)(2,1)} async-done(((bf16[2,128,512]{2,1,0:T(8,128)(2,1)}), bf16[2,128,512]{2,1,0:T(8,128)(2,1)}) %all-reduce.2.cloned.1.call-update) | async-done | bytes 262160 | tf_op jit(solution)/shard_map/psum | solution.py:122
  204.6 1.8 convert_element_type.134
  (74 shorter events, 0.7 us)
Async XLA Ops:
  7.2 32.7 %copy-start = (bf16[1,1,12,128,128]{4,3,2,1,0:T(8,128)(2,1)S(1)}, bf16[1,1,12,128,128]{4,3,2,1,0:T(8,128)(2,1)}, u32[]{:S(2)}) copy-start(bf16[1,1,12,128,128]{4,3,2,1,0:T(8,128)(2,1)} %param.12) | copy-start | bytes 1179652
  7.2 51.5 %reduce-scatter.4.cloned.1.call-start = ((), (), s32[]{:S(2)}) async-start(), calls=%async_computation.3 | async-start | bytes 786432 | tf_op jit(solution)/shard_map/reduce_scatter | solution.py:78
  8.2 9.4 %collective-permute-start = (bf16[1,1,128,512]{3,2,1,0:T(8,128)(2,1)S(1)}, bf16[1,1,128,512]{3,2,1,0:T(8,128)(2,1)S(1)}, u32[]{:S(2)}, u32[]{:S(2)}) collective-permute-start(bf16[1,1,128,512]{3,2,1,0:T(8,128)(2,1)S(1)} %slice.89), channel_id=1, source_target_pairs={{0,4},{4,8},{8,12},{12,0},{1,5},{5,9},{9,13},{13,1},{2,6},{6,10},{... | collective-permute-start | bytes 393224 | tf_op jit(solution)/shard_map/ppermute | solution.py:14
  11.3 7.8 %collective-permute-start.1 = (bf16[1,1,128,512]{3,2,1,0:T(8,128)(2,1)S(1)}, bf16[1,1,128,512]{3,2,1,0:T(8,128)(2,1)S(1)}, u32[]{:S(2)}, u32[]{:S(2)}) collective-permute-start(bf16[1,1,128,512]{3,2,1,0:T(8,128)(2,1)S(1)} %slice.89), channel_id=1, source_target_pairs={{4,0},{8,4},{12,8},{0,12},{5,1},{9,5},{13,9},{1,13},{6,2},{10,6},{... | collective-permute-start | bytes 393224 | tf_op jit(solution)/shard_map/ppermute | solution.py:17
  14.7 25.2 %copy-start.16 = (pred[12]{0:T(512)(128)(4,1)}, pred[12]{0:T(512)(128)(4,1)S(1)}, u32[]{:S(2)}) copy-start(pred[12]{0:T(512)(128)(4,1)S(1)} %compare_and_fusion) | copy-start | bytes 40
  19.1 12.1 %collective-permute-start.2 = (bf16[3,1,128,512]{3,2,1,0:T(8,128)(2,1)S(1)}, bf16[3,1,128,512]{3,2,1,0:T(8,128)(2,1)S(1)}, u32[]{:S(2)}, u32[]{:S(2)}) collective-permute-start(bf16[3,1,128,512]{3,2,1,0:T(8,128)(2,1)S(1)} %pad_maximum_fusion.1), channel_id=1, source_target_pairs={{0,2},{2,0},{1,3},{3,1},{4,6},{6,4},{5,7},{7,5},{8,10},{10,8},{9,1... | collective-permute-start | bytes 1179656 | tf_op jit(solution)/shard_map/ppermute | solution.py:14
  20.6 17.4 %collective-permute-start.3 = (bf16[3,1,128,512]{3,2,1,0:T(8,128)(2,1)S(1)}, bf16[3,1,128,512]{3,2,1,0:T(8,128)(2,1)S(1)}, u32[]{:S(2)}, u32[]{:S(2)}) collective-permute-start(bf16[3,1,128,512]{3,2,1,0:T(8,128)(2,1)S(1)} %pad_maximum_fusion.1), channel_id=1, source_target_pairs={{2,0},{0,2},{3,1},{1,3},{6,4},{4,6},{7,5},{5,7},{10,8},{8,10},{11,... | collective-permute-start | bytes 1179656 | tf_op jit(solution)/shard_map/ppermute | solution.py:17
  42.0 3.5 %copy-start.15 = (s32[1,1,12]{2,1,0:T(1,128)S(1)}, s32[1,1,12]{2,1,0:T(1,128)}, u32[]{:S(2)}) copy-start(s32[1,1,12]{2,1,0:T(1,128)} %param.14) | copy-start | bytes 148
  49.3 1.0 copy-start.14
  50.2 59.1 %reduce-scatter.6.cloned.1.call-start = ((), (), s32[]{:S(2)}) async-start(), calls=%async_computation.4 | async-start | bytes 786432 | tf_op jit(solution)/shard_map/reduce_scatter | solution.py:78
  52.6 4.7 %copy-start.6 = (bf16[2,512,512]{2,1,0:T(8,128)(2,1)S(1)}, bf16[2,512,512]{2,1,0:T(8,128)(2,1)}, u32[]{:S(2)}) copy-start(bf16[2,512,512]{2,1,0:T(8,128)(2,1)} %param.15) | copy-start | bytes 3145732
  61.1 21.6 %copy-start.2 = (bf16[256,512]{1,0:T(8,128)(2,1)}, bf16[256,512]{1,0:T(8,128)(2,1)S(1)}, u32[]{:S(2)}) copy-start(bf16[256,512]{1,0:T(8,128)(2,1)S(1)} %get-tuple-element.19) | copy-start | bytes 786436
  61.1 8.3 %collective-permute-start.4 = (bf16[1,1,128,512]{3,2,1,0:T(8,128)(2,1)S(1)}, bf16[1,1,128,512]{3,2,1,0:T(8,128)(2,1)S(1)}, u32[]{:S(2)}, u32[]{:S(2)}) collective-permute-start(bf16[1,1,128,512]{3,2,1,0:T(8,128)(2,1)S(1)} %slice_bitcast_fusion.6), channel_id=1, source_target_pairs={{0,4},{4,8},{8,12},{12,0},{1,5},{5,9},{9,13},{13,1},{2,6},{6,10},{... | collective-permute-start | bytes 393224 | tf_op jit(solution)/shard_map/ppermute | solution.py:14
  62.9 7.6 %collective-permute-start.5 = (bf16[1,1,128,512]{3,2,1,0:T(8,128)(2,1)S(1)}, bf16[1,1,128,512]{3,2,1,0:T(8,128)(2,1)S(1)}, u32[]{:S(2)}, u32[]{:S(2)}) collective-permute-start(bf16[1,1,128,512]{3,2,1,0:T(8,128)(2,1)S(1)} %slice_bitcast_fusion.6), channel_id=1, source_target_pairs={{4,0},{8,4},{12,8},{0,12},{5,1},{9,5},{13,9},{1,13},{6,2},{10,6},{... | collective-permute-start | bytes 393224 | tf_op jit(solution)/shard_map/ppermute | solution.py:17
  70.5 12.1 %collective-permute-start.6 = (bf16[3,1,128,512]{3,2,1,0:T(8,128)(2,1)S(1)}, bf16[3,1,128,512]{3,2,1,0:T(8,128)(2,1)S(1)}, u32[]{:S(2)}, u32[]{:S(2)}) collective-permute-start(bf16[3,1,128,512]{3,2,1,0:T(8,128)(2,1)S(1)} %pad_maximum_fusion.2), channel_id=1, source_target_pairs={{0,2},{2,0},{1,3},{3,1},{4,6},{6,4},{5,7},{7,5},{8,10},{10,8},{9,1... | collective-permute-start | bytes 1179656 | tf_op jit(solution)/shard_map/ppermute | solution.py:14
  72.0 17.5 %collective-permute-start.7 = (bf16[3,1,128,512]{3,2,1,0:T(8,128)(2,1)S(1)}, bf16[3,1,128,512]{3,2,1,0:T(8,128)(2,1)S(1)}, u32[]{:S(2)}, u32[]{:S(2)}) collective-permute-start(bf16[3,1,128,512]{3,2,1,0:T(8,128)(2,1)S(1)} %pad_maximum_fusion.2), channel_id=1, source_target_pairs={{2,0},{0,2},{3,1},{1,3},{6,4},{4,6},{7,5},{5,7},{10,8},{8,10},{11,... | collective-permute-start | bytes 1179656 | tf_op jit(solution)/shard_map/ppermute | solution.py:17
  101.8 70.0 %reduce-scatter.8.cloned.1.call-start = ((), (), s32[]{:S(2)}) async-start(), calls=%async_computation.5 | async-start | bytes 1310720 | tf_op jit(solution)/shard_map/reduce_scatter | solution.py:121
  103.7 5.6 %copy-start.3 = (bf16[256,512]{1,0:T(8,128)(2,1)S(1)}, bf16[256,512]{1,0:T(8,128)(2,1)}, u32[]{:S(2)}) copy-start(bf16[256,512]{1,0:T(8,128)(2,1)} %copy-done.2) | copy-start | bytes 786436
  103.7 5.6 %copy-start.17 = (f32[256]{0:T(256)S(1)}, f32[256]{0:T(256)}, u32[]{:S(2)}) copy-start(f32[256]{0:T(256)} %compare_convert_fusion.1) | copy-start | bytes 3076
  103.7 5.6 %copy-start.19 = (bf16[1,1,256,512]{3,2,1,0:T(8,128)(2,1)S(1)}, bf16[1,1,256,512]{3,2,1,0:T(8,128)(2,1)}, u32[]{:S(2)}) copy-start(bf16[1,1,256,512]{3,2,1,0:T(8,128)(2,1)} %param.11) | copy-start | bytes 786436
  105.2 6.4 %copy-start.7 = (bf16[2,512,512]{2,1,0:T(8,128)(2,1)S(1)}, bf16[2,512,512]{2,1,0:T(8,128)(2,1)}, u32[]{:S(2)}) copy-start(bf16[2,512,512]{2,1,0:T(8,128)(2,1)} %multiply_convert_fusion) | copy-start | bytes 3145732
  111.7 5.3 %copy-start.12 = (bf16[256,512]{1,0:T(8,128)(2,1)}, bf16[256,512]{1,0:T(8,128)(2,1)S(1)}, u32[]{:S(2)}) copy-start(bf16[256,512]{1,0:T(8,128)(2,1)S(1)} %get-tuple-element.13) | copy-start | bytes 786436
  112.0 0.7 copy-start.9
  119.1 3.5 %copy-start.18 = (s32[1,1,12]{2,1,0:T(1,128)S(1)}, s32[1,1,12]{2,1,0:T(1,128)}, u32[]{:S(2)}) copy-start(s32[1,1,12]{2,1,0:T(1,128)} %param.13) | copy-start | bytes 148
  127.3 9.1 %copy-start.1 = (f32[512,512]{1,0:T(8,128)S(1)}, f32[512,512]{1,0:T(8,128)}, u32[]{:S(2)}) copy-start(f32[512,512]{1,0:T(8,128)} %squeeze.39) | copy-start | bytes 3145732
  127.3 9.1 %copy-start.4 = (bf16[256,512]{1,0:T(8,128)(2,1)S(1)}, bf16[256,512]{1,0:T(8,128)(2,1)}, u32[]{:S(2)}) copy-start(bf16[256,512]{1,0:T(8,128)(2,1)} %copy-done.2) | copy-start | bytes 786436
  127.3 9.1 %copy-start.11 = (bf16[256,512]{1,0:T(8,128)(2,1)S(1)}, bf16[256,512]{1,0:T(8,128)(2,1)}, u32[]{:S(2)}) copy-start(bf16[256,512]{1,0:T(8,128)(2,1)} %reduce-scatter.6.cloned.1.call-done) | copy-start | bytes 786436
  127.3 9.0 %copy-start.13 = (bf16[256,512]{1,0:T(8,128)(2,1)S(1)}, bf16[256,512]{1,0:T(8,128)(2,1)}, u32[]{:S(2)}) copy-start(bf16[256,512]{1,0:T(8,128)(2,1)} %copy-done.12) | copy-start | bytes 786436
  127.4 9.4 %collective-permute-start.10 = (bf16[1,128,512]{2,1,0:T(8,128)(2,1)S(1)}, bf16[1,128,512]{2,1,0:T(8,128)(2,1)S(1)}, u32[]{:S(2)}, u32[]{:S(2)}) collective-permute-start(bf16[1,128,512]{2,1,0:T(8,128)(2,1)S(1)} %get-tuple-element.9), channel_id=1, source_target_pairs={{0,2},{1,3},{4,6},{5,7},{8,10},{9,11},{12,14},{13,15},{16,18},{17,... | collective-permute-start | bytes 393224 | tf_op jit(solution)/shard_map/ppermute | solution.py:14
  131.1 7.3 %collective-permute-start.11 = (bf16[1,128,512]{2,1,0:T(8,128)(2,1)S(1)}, bf16[1,128,512]{2,1,0:T(8,128)(2,1)S(1)}, u32[]{:S(2)}, u32[]{:S(2)}) collective-permute-start(bf16[1,128,512]{2,1,0:T(8,128)(2,1)S(1)} %get-tuple-element.8), channel_id=1, source_target_pairs={{2,0},{3,1},{6,4},{7,5},{10,8},{11,9},{14,12},{15,13},{18,16},{19,... | collective-permute-start | bytes 393224 | tf_op jit(solution)/shard_map/ppermute | solution.py:17
  132.4 8.2 %collective-permute-start.8 = (bf16[1,128,512]{2,1,0:T(8,128)(2,1)S(1)}, bf16[1,128,512]{2,1,0:T(8,128)(2,1)S(1)}, u32[]{:S(2)}, u32[]{:S(2)}) collective-permute-start(bf16[1,128,512]{2,1,0:T(8,128)(2,1)S(1)} %get-tuple-element.7), channel_id=1, source_target_pairs={{0,4},{4,8},{8,12},{12,0},{1,5},{5,9},{9,13},{13,1},{2,6},{6,10},{... | collective-permute-start | bytes 393224 | tf_op jit(solution)/shard_map/ppermute | solution.py:14
  134.0 8.0 %collective-permute-start.9 = (bf16[1,128,512]{2,1,0:T(8,128)(2,1)S(1)}, bf16[1,128,512]{2,1,0:T(8,128)(2,1)S(1)}, u32[]{:S(2)}, u32[]{:S(2)}) collective-permute-start(bf16[1,128,512]{2,1,0:T(8,128)(2,1)S(1)} %get-tuple-element.10), channel_id=1, source_target_pairs={{4,0},{8,4},{12,8},{0,12},{5,1},{9,5},{13,9},{1,13},{6,2},{10,6},{... | collective-permute-start | bytes 393224 | tf_op jit(solution)/shard_map/ppermute | solution.py:17
  136.3 5.7 %copy-start.22 = (f32[256,512]{1,0:T(8,128)S(1)}, f32[256,512]{1,0:T(8,128)}, u32[]{:S(2)}) copy-start(f32[256,512]{1,0:T(8,128)} %get-tuple-element.20) | copy-start | bytes 1572868
  136.7 5.4 %copy-start.5 = (f32[512,512]{1,0:T(8,128)S(1)}, f32[512,512]{1,0:T(8,128)}, u32[]{:S(2)}) copy-start(f32[512,512]{1,0:T(8,128)} %squeeze.38) | copy-start | bytes 3145732
  136.7 5.4 %copy-start.8 = (bf16[1,1,256,512]{3,2,1,0:T(8,128)(2,1)S(1)}, bf16[1,1,256,512]{3,2,1,0:T(8,128)(2,1)}, u32[]{:S(2)}) copy-start(bf16[1,1,256,512]{3,2,1,0:T(8,128)(2,1)} %param.10) | copy-start | bytes 786436
  136.7 5.4 %copy-start.10 = (bf16[256,512]{1,0:T(8,128)(2,1)S(1)}, bf16[256,512]{1,0:T(8,128)(2,1)}, u32[]{:S(2)}) copy-start(bf16[256,512]{1,0:T(8,128)(2,1)} %copy-done.9) | copy-start | bytes 786436
  136.7 5.4 %copy-start.20 = (bf16[1,1,256,512]{3,2,1,0:T(8,128)(2,1)S(1)}, bf16[1,1,256,512]{3,2,1,0:T(8,128)(2,1)}, u32[]{:S(2)}) copy-start(bf16[1,1,256,512]{3,2,1,0:T(8,128)(2,1)} %param.11) | copy-start | bytes 786436
  136.7 5.4 %copy-start.21 = (bf16[256,512]{1,0:T(8,128)(2,1)S(1)}, bf16[256,512]{1,0:T(8,128)(2,1)}, u32[]{:S(2)}) copy-start(bf16[256,512]{1,0:T(8,128)(2,1)} %reduce-scatter.4.cloned.1.call-done) | copy-start | bytes 786436
  143.8 60.8 %all-reduce.2.cloned.1.call-start = ((), (), s32[]{:S(2)}) async-start(), calls=%async_computation.6 | async-start | bytes 524288 | tf_op jit(solution)/shard_map/psum | solution.py:122
Sparse Core Ops, SparseCore 0:
  50.3 7.6 reduce-scatter.3
  101.9 7.3 reduce-scatter.5
  143.9 27.7 reduce-scatter.7
  174.0 30.5 all-reduce.1
where the time goes:
time: 214 us; the launch traced here: 213 us
  waiting for transfers between devices  113 us (53%)
  local copies, waits for them, and re-layouts  29.8 us (14%)
  matrix products  23.7 us (11%)
  starting transfers between devices  22.3 us (10%)
  between operations  14.9 us (7%)
  other arithmetic  7.39 us (3%)
  blocking collectives  2.35 us (1%)
    psum x1, waiting for transfers between devices, body(): result = lax.psum(shares, ('eta', 'half')).astype(jnp.float32)  32.9 us
    ppermute x6, waiting for transfers between devices, with_halo(): lax.ppermute(lax.slice_in_dim(block, block.shape[dim] - width, None, axis...  28.5 us
    reduce_scatter x1, waiting for transfers between devices, body(): lax.psum_scatter(stacked.astype(jnp.bfloat16), 'phi', scatter_dimension=1...  27.9 us
    ppermute x6, waiting for transfers between devices, with_halo(): lax.ppermute(lax.slice_in_dim(block, 0, width, axis=dim), axis, backward)  19.2 us
    ppermute x6, starting transfers between devices, with_halo(): lax.ppermute(lax.slice_in_dim(block, block.shape[dim] - width, None, axis...  13.3 us
    ppermute x6, starting transfers between devices, with_halo(): lax.ppermute(lax.slice_in_dim(block, 0, width, axis=dim), axis, backward)  8.89 us
    dot_general x2, matrix products, body(): jnp.einsum('bt,tid->bid', messages_onehot, messages_parts, precision=lax....  7.58 us
    dot_general x2, local copies, waits for them, and re-layouts, body(): jnp.einsum('tij,tjd->tid', tile_set, messages_picked, preferred_element_t...  6.92 us
  transfers between devices with their start and end apart: 16, of which 14 were waited for; matrix products, arithmetic and copies ran while one was open for 7% of the time, Pallas kernels for 0%

commit v1 on v0

--- a/solution.py
+++ b/solution.py
@@ -119,7 +119,7 @@
             upstream = live * upstream + back.astype(jnp.float32) + own
     stacked = jnp.stack(partials)
     shares = lax.psum_scatter(stacked.astype(jnp.bfloat16), "phi", scatter_dimension=1, tiled=True)
-    result = lax.psum(shares, ("eta", "half")).astype(jnp.float32)
+    result = lax.psum(lax.psum(shares, "half"), "eta").astype(jnp.float32)
     return (state[None, None], result)
 
 

time: 214 us -> 226 us (1.056)
  waiting for transfers between devices: 113 us -> 125 us
    psum x1 -> x2, waiting for transfers between devices: 32.9 us -> 45.7 us  [body(): result = lax.psum(lax.psum(shares, 'half'), 'eta').astype(jnp.float32)]
  transfers between devices with their start and end apart: 16 -> 17, of which waited for: 14 -> 15; matrix products, arithmetic and copies ran while one was open for 7% -> 6% of each run, Pallas kernels for 0% -> 0%
where the time goes in v1:
time: 226 us
  waiting for transfers between devices  125 us (55%)
  local copies, waits for them, and re-layouts  29.8 us (13%)
  matrix products  23.7 us (10%)
  starting transfers between devices  22.4 us (10%)
  between operations  14.9 us (7%)
  other arithmetic  7.39 us (3%)
  blocking collectives  2.35 us (1%)
    psum x2, waiting for transfers between devices, body(): result = lax.psum(lax.psum(shares, 'half'), 'eta').astype(jnp.float32)  45.7 us
    ppermute x6, waiting for transfers between devices, with_halo(): lax.ppermute(lax.slice_in_dim(block, block.shape[dim] - width, None, axis...  28.5 us
    reduce_scatter x1, waiting for transfers between devices, body(): lax.psum_scatter(stacked.astype(jnp.bfloat16), 'phi', scatter_dimension=1...  27.9 us
    ppermute x6, waiting for transfers between devices, with_halo(): lax.ppermute(lax.slice_in_dim(block, 0, width, axis=dim), axis, backward)  19.2 us
    ppermute x6, starting transfers between devices, with_halo(): lax.ppermute(lax.slice_in_dim(block, block.shape[dim] - width, None, axis...  13.3 us
    ppermute x6, starting transfers between devices, with_halo(): lax.ppermute(lax.slice_in_dim(block, 0, width, axis=dim), axis, backward)  8.89 us
    dot_general x2, matrix products, body(): jnp.einsum('bt,tid->bid', messages_onehot, messages_parts, precision=lax....  7.58 us
    dot_general x2, local copies, waits for them, and re-layouts, body(): jnp.einsum('tij,tjd->tid', tile_set, messages_picked, preferred_element_t...  6.92 us
  transfers between devices with their start and end apart: 17, of which 15 were waited for; matrix products, arithmetic and copies ran while one was open for 6% of the time, Pallas kernels for 0%

profile of v1, /device:TPU:0, one launch (start us, length us, event | category | flops | bytes accessed | tf_op | source)
XLA Modules:
  0.0 225.8 jit_solution(17761203293222671230)
XLA Ops:
  7.2 1.0 slice.89
  8.2 3.1 %collective-permute-start = (bf16[1,1,128,512]{3,2,1,0:T(8,128)(2,1)S(1)}, bf16[1,1,128,512]{3,2,1,0:T(8,128)(2,1)S(1)}, u32[]{:S(2)}, u32[]{:S(2)}) collective-permute-start(bf16[1,1,128,512]{3,2,1,0:T(8,128)(2,1)S(1)} %slice.89), channel_id=1, source_target_pairs={{0,4},{4,8},{8,12},{12,0},{1,5},{5,9},{9,13},{13,1},{2,6},{6,10},{... | collective-permute-start | bytes 393224 | tf_op jit(solution)/shard_map/ppermute | solution.py:14
  11.3 2.1 collective-permute-start.1
  13.4 0.7 compare_select_fusion
  14.0 0.7 compare_and_fusion
  14.7 1.0 constant_dynamic-update-slice_fusion
  15.7 1.9 collective-permute-done
  17.6 1.4 collective-permute-done.1
  19.1 1.6 collective-permute-start.2
  20.6 0.5 collective-permute-start.3
  21.2 10.0 %collective-permute-done.2 = bf16[3,1,128,512]{3,2,1,0:T(8,128)(2,1)S(1)} collective-permute-done((bf16[3,1,128,512]{3,2,1,0:T(8,128)(2,1)S(1)}, bf16[3,1,128,512]{3,2,1,0:T(8,128)(2,1)S(1)}, u32[]{:S(2)}, u32[]{:S(2)}) %collective-permute-start.2) | collective-permute-done | bytes 393248 | tf_op jit(solution)/shard_map/ppermute | solution.py:14
  31.2 6.8 %collective-permute-done.3 = bf16[3,1,128,512]{3,2,1,0:T(8,128)(2,1)S(1)} collective-permute-done((bf16[3,1,128,512]{3,2,1,0:T(8,128)(2,1)S(1)}, bf16[3,1,128,512]{3,2,1,0:T(8,128)(2,1)S(1)}, u32[]{:S(2)}, u32[]{:S(2)}) %collective-permute-start.3) | collective-permute-done | bytes 393248 | tf_op jit(solution)/shard_map/ppermute | solution.py:17
  38.0 1.9 gather_fusion.1
  39.9 2.1 fusion.8
  42.0 3.5 %copy.19 = f32[12,512,128]{1,0,2:T(8,128)} copy(f32[12,512,128]{2,1,0:T(8,128)S(1)} %fusion.8) | data formatting | bytes 6291456 | tf_op jit(solution)/shard_map/tij,tjd->tid/dot_general | solution.py:70
  45.5 3.8 %fusion.16 = bf16[4,128,512]{2,0,1:T(4,128)(2,1)S(1)} fusion(f32[12,512,128]{1,0,2:T(8,128)} %copy.19, s32[12]{0:T(128)S(1)} %bitcast.122), kind=kOutput, calls=%fused_computation.22 | convolution fusion | flops 38010928 | bytes 3670064 | tf_op jit(solution)/shard_map/bt,tid->bid/dot_general | solution.py:74
  49.3 0.9 copy.14
  50.3 2.3 %broadcast_in_dim.41 = f32[2,8,64,8,64]{4,3,2,1,0:T(8,128)} broadcast(f32[2,8,8]{2,1,0:T(8,128)S(1)} %convert_element_type.115), dimensions={0,1,3} | broadcast | bytes 2097664 | tf_op jit(solution)/shard_map/broadcast_in_dim | solution.py:49
  52.6 3.5 %convert_element_type.116 = f32[2,512,512]{2,1,0:T(8,128)S(1)} reshape(f32[2,8,64,8,64]{4,3,2,1,0:T(8,128)} %broadcast_in_dim.41) | data formatting | bytes 4194304 | tf_op jit(solution)/shard_map/convert_element_type | solution.py:51
  56.8 0.6 compare_convert_fusion.1
  57.3 1.3 multiply_convert_fusion
  58.7 2.4 %fusion.35 = (bf16[256,512]{1,0:T(8,128)(2,1)S(1)}, f32[256,512]{1,0:T(8,128)}) fusion(bf16[1,1,256,512]{3,2,1,0:T(8,128)(2,1)} %param.10, f32[256]{0:T(256)} %compare_convert_fusion.1, bf16[2,512,512]{2,1,0:T(8,128)(2,1)} %multiply_convert_fusion, bf16[256,512]{1,0:T(8,128)(2,1)} %reduce-scatter.4.cloned.1.call-done), kind=kOutput, calls=%fused_computation.43 | convolution fusion | flops 135790592 | bytes 2098176 | tf_op jit(solution)/shard_map/dot_general | solution.py:83
  61.1 1.8 collective-permute-start.4
  62.9 2.1 collective-permute-start.5
  65.0 4.4 %collective-permute-done.4 = bf16[1,1,128,512]{3,2,1,0:T(8,128)(2,1)S(1)} collective-permute-done((bf16[1,1,128,512]{3,2,1,0:T(8,128)(2,1)S(1)}, bf16[1,1,128,512]{3,2,1,0:T(8,128)(2,1)S(1)}, u32[]{:S(2)}, u32[]{:S(2)}) %collective-permute-start.4) | collective-permute-done | bytes 131104 | tf_op jit(solution)/shard_map/ppermute | solution.py:14
  69.4 1.1 collective-permute-done.5
  70.5 1.5 collective-permute-start.6
  72.0 0.6 collective-permute-start.7
  72.6 10.0 %collective-permute-done.6 = bf16[3,1,128,512]{3,2,1,0:T(8,128)(2,1)S(1)} collective-permute-done((bf16[3,1,128,512]{3,2,1,0:T(8,128)(2,1)S(1)}, bf16[3,1,128,512]{3,2,1,0:T(8,128)(2,1)S(1)}, u32[]{:S(2)}, u32[]{:S(2)}) %collective-permute-start.6) | collective-permute-done | bytes 393248 | tf_op jit(solution)/shard_map/ppermute | solution.py:14
  82.7 6.9 %collective-permute-done.7 = bf16[3,1,128,512]{3,2,1,0:T(8,128)(2,1)S(1)} collective-permute-done((bf16[3,1,128,512]{3,2,1,0:T(8,128)(2,1)S(1)}, bf16[3,1,128,512]{3,2,1,0:T(8,128)(2,1)S(1)}, u32[]{:S(2)}, u32[]{:S(2)}) %collective-permute-start.7) | collective-permute-done | bytes 393248 | tf_op jit(solution)/shard_map/ppermute | solution.py:17
  89.6 1.9 gather_fusion.2
  91.5 2.1 fusion.6
  93.6 3.5 %copy.20 = f32[12,512,128]{1,0,2:T(8,128)} copy(f32[12,512,128]{2,1,0:T(8,128)S(1)} %fusion.6) | data formatting | bytes 6291456 | tf_op jit(solution)/shard_map/tij,tjd->tid/dot_general | solution.py:70
  97.1 3.8 %fusion.19 = bf16[4,128,512]{2,0,1:T(4,128)(2,1)S(1)} fusion(f32[12,512,128]{1,0,2:T(8,128)} %copy.20, s32[12]{0:T(128)S(1)} %bitcast.123), kind=kOutput, calls=%fused_computation.23 | convolution fusion | flops 38010928 | bytes 3670064 | tf_op jit(solution)/shard_map/bt,tid->bid/dot_general | solution.py:74
  100.9 0.9 copy.15
  101.8 0.2 broadcast_in_dim.46
  102.0 1.5 squeeze.38
  103.5 0.2 broadcast_in_dim.47
  103.8 1.5 squeeze.39
  105.3 4.0 %reduce-scatter.6.cloned.1.call-done = bf16[256,512]{1,0:T(8,128)(2,1)} async-done(((bf16[512,512]{1,0:T(8,128)(2,1)}), bf16[256,512]{1,0:T(8,128)(2,1)}) %reduce-scatter.6.cloned.1.call-update) | async-done | bytes 262160 | tf_op jit(solution)/shard_map/reduce_scatter | solution.py:78
  109.3 2.4 %fusion.42 = (bf16[256,512]{1,0:T(8,128)(2,1)S(1)}, bf16[1,1,256,512]{3,2,1,0:T(8,128)(2,1)}) fusion(bf16[1,1,256,512]{3,2,1,0:T(8,128)(2,1)S(1)} %copy-done.19, f32[256]{0:T(256)S(1)} %copy-done.17, bf16[256,512]{1,0:T(8,128)(2,1)S(1)} %copy-done.3, bf16[2,512,512]{2,1,0:T(8,128)(2,1)} %multiply_convert_fusion, ...), kind=kOutput, calls=%fused_computation.54 | convolution fusion | flops 136839168 | bytes 2098176 | tf_op jit(solution)/shard_map/dot_general | solution.py:83
  111.7 0.3 convolution_convert_fusion
  112.0 0.7 copy-done.9
  112.7 2.3 %all_gather.3 = bf16[512,512]{1,0:T(8,128)(2,1)S(1)} all-gather(bf16[256,512]{1,0:T(8,128)(2,1)S(1)} %convolution_convert_fusion), channel_id=1, replica_groups=mesh['group'=2,'phi'=4,'eta'=2,'half'=2] {'half'}, dimensions={0}, use_global_device_ids=true | all-gather | bytes 786432 | tf_op jit(solution)/shard_map/all_gather | solution.py:99
  115.1 1.9 gather_fusion
  116.9 2.1 fusion.10
  119.1 3.5 %copy.21 = f32[12,512,128]{1,0,2:T(8,128)} copy(f32[12,512,128]{2,1,0:T(8,128)S(1)} %fusion.10) | data formatting | bytes 6291456 | tf_op jit(solution)/shard_map/tji,tjd->tid/dot_general | solution.py:107
  122.6 3.7 %fusion = f32[6,128,512]{2,0,1:T(8,128)S(1)} fusion(f32[12,512,128]{1,0,2:T(8,128)} %copy.21, s32[12]{0:T(128)S(1)} %bitcast.124), kind=kOutput, calls=%fused_computation.3 | convolution fusion | flops 56623176 | bytes 4718640 | tf_op jit(solution)/shard_map/st,tid->sid/dot_general | solution.py:109
  126.3 0.9 fusion.80
  127.4 3.8 %collective-permute-start.10 = (bf16[1,128,512]{2,1,0:T(8,128)(2,1)S(1)}, bf16[1,128,512]{2,1,0:T(8,128)(2,1)S(1)}, u32[]{:S(2)}, u32[]{:S(2)}) collective-permute-start(bf16[1,128,512]{2,1,0:T(8,128)(2,1)S(1)} %get-tuple-element.9), channel_id=1, source_target_pairs={{0,2},{1,3},{4,6},{5,7},{8,10},{9,11},{12,14},{13,15},{16,18},{17,... | collective-permute-start | bytes 393224 | tf_op jit(solution)/shard_map/ppermute | solution.py:14
  131.1 1.3 collective-permute-start.11
  132.4 1.5 collective-permute-start.8
  134.0 2.3 %collective-permute-start.9 = (bf16[1,128,512]{2,1,0:T(8,128)(2,1)S(1)}, bf16[1,128,512]{2,1,0:T(8,128)(2,1)S(1)}, u32[]{:S(2)}, u32[]{:S(2)}) collective-permute-start(bf16[1,128,512]{2,1,0:T(8,128)(2,1)S(1)} %get-tuple-element.10), channel_id=1, source_target_pairs={{4,0},{8,4},{12,8},{0,12},{5,1},{9,5},{13,9},{1,13},{6,2},{10,6},{... | collective-permute-start | bytes 393224 | tf_op jit(solution)/shard_map/ppermute | solution.py:17
  136.3 0.3 fusion.24
  136.7 1.7 collective-permute-done.11
  138.5 2.2 collective-permute-done.8
  140.7 1.3 collective-permute-done.9
  141.9 0.1 fusion.50
  142.1 0.6 fusion.25
  142.7 1.1 pad_maximum_fusion
  143.9 27.9 %reduce-scatter.8.cloned.1.call-done = bf16[2,128,512]{2,1,0:T(8,128)(2,1)} async-done(((bf16[2,512,512]{2,1,0:T(8,128)(2,1)}), bf16[2,128,512]{2,1,0:T(8,128)(2,1)}) %reduce-scatter.8.cloned.1.call-update) | async-done | bytes 262160 | tf_op jit(solution)/shard_map/reduce_scatter | solution.py:121
  171.8 19.2 %all-reduce.3.cloned.1.call-done = bf16[2,128,512]{2,1,0:T(8,128)(2,1)} async-done(((bf16[2,128,512]{2,1,0:T(8,128)(2,1)}), bf16[2,128,512]{2,1,0:T(8,128)(2,1)}) %all-reduce.3.cloned.1.call-update) | async-done | bytes 262160 | tf_op jit(solution)/shard_map/psum | solution.py:122
  191.0 26.5 %all-reduce.5.cloned.1.call-done = bf16[2,128,512]{2,1,0:T(8,128)(2,1)} async-done(((bf16[2,128,512]{2,1,0:T(8,128)(2,1)}), bf16[2,128,512]{2,1,0:T(8,128)(2,1)}) %all-reduce.5.cloned.1.call-update) | async-done | bytes 262160 | tf_op jit(solution)/shard_map/psum | solution.py:122
  217.5 1.8 convert_element_type.134
  (77 shorter events, 0.8 us)
Async XLA Ops:
  7.2 32.7 %copy-start = (bf16[1,1,12,128,128]{4,3,2,1,0:T(8,128)(2,1)S(1)}, bf16[1,1,12,128,128]{4,3,2,1,0:T(8,128)(2,1)}, u32[]{:S(2)}) copy-start(bf16[1,1,12,128,128]{4,3,2,1,0:T(8,128)(2,1)} %param.12) | copy-start | bytes 1179652
  7.2 51.5 %reduce-scatter.4.cloned.1.call-start = ((), (), s32[]{:S(2)}) async-start(), calls=%async_computation.3 | async-start | bytes 786432 | tf_op jit(solution)/shard_map/reduce_scatter | solution.py:78
  8.2 9.4 %collective-permute-start = (bf16[1,1,128,512]{3,2,1,0:T(8,128)(2,1)S(1)}, bf16[1,1,128,512]{3,2,1,0:T(8,128)(2,1)S(1)}, u32[]{:S(2)}, u32[]{:S(2)}) collective-permute-start(bf16[1,1,128,512]{3,2,1,0:T(8,128)(2,1)S(1)} %slice.89), channel_id=1, source_target_pairs={{0,4},{4,8},{8,12},{12,0},{1,5},{5,9},{9,13},{13,1},{2,6},{6,10},{... | collective-permute-start | bytes 393224 | tf_op jit(solution)/shard_map/ppermute | solution.py:14
  11.3 7.8 %collective-permute-start.1 = (bf16[1,1,128,512]{3,2,1,0:T(8,128)(2,1)S(1)}, bf16[1,1,128,512]{3,2,1,0:T(8,128)(2,1)S(1)}, u32[]{:S(2)}, u32[]{:S(2)}) collective-permute-start(bf16[1,1,128,512]{3,2,1,0:T(8,128)(2,1)S(1)} %slice.89), channel_id=1, source_target_pairs={{4,0},{8,4},{12,8},{0,12},{5,1},{9,5},{13,9},{1,13},{6,2},{10,6},{... | collective-permute-start | bytes 393224 | tf_op jit(solution)/shard_map/ppermute | solution.py:17
  14.7 25.2 %copy-start.16 = (pred[12]{0:T(512)(128)(4,1)}, pred[12]{0:T(512)(128)(4,1)S(1)}, u32[]{:S(2)}) copy-start(pred[12]{0:T(512)(128)(4,1)S(1)} %compare_and_fusion) | copy-start | bytes 40
  19.1 12.1 %collective-permute-start.2 = (bf16[3,1,128,512]{3,2,1,0:T(8,128)(2,1)S(1)}, bf16[3,1,128,512]{3,2,1,0:T(8,128)(2,1)S(1)}, u32[]{:S(2)}, u32[]{:S(2)}) collective-permute-start(bf16[3,1,128,512]{3,2,1,0:T(8,128)(2,1)S(1)} %pad_maximum_fusion.1), channel_id=1, source_target_pairs={{0,2},{2,0},{1,3},{3,1},{4,6},{6,4},{5,7},{7,5},{8,10},{10,8},{9,1... | collective-permute-start | bytes 1179656 | tf_op jit(solution)/shard_map/ppermute | solution.py:14
  20.6 17.4 %collective-permute-start.3 = (bf16[3,1,128,512]{3,2,1,0:T(8,128)(2,1)S(1)}, bf16[3,1,128,512]{3,2,1,0:T(8,128)(2,1)S(1)}, u32[]{:S(2)}, u32[]{:S(2)}) collective-permute-start(bf16[3,1,128,512]{3,2,1,0:T(8,128)(2,1)S(1)} %pad_maximum_fusion.1), channel_id=1, source_target_pairs={{2,0},{0,2},{3,1},{1,3},{6,4},{4,6},{7,5},{5,7},{10,8},{8,10},{11,... | collective-permute-start | bytes 1179656 | tf_op jit(solution)/shard_map/ppermute | solution.py:17
  42.0 3.5 %copy-start.15 = (s32[1,1,12]{2,1,0:T(1,128)S(1)}, s32[1,1,12]{2,1,0:T(1,128)}, u32[]{:S(2)}) copy-start(s32[1,1,12]{2,1,0:T(1,128)} %param.14) | copy-start | bytes 148
  49.3 1.0 copy-start.14
  50.2 59.1 %reduce-scatter.6.cloned.1.call-start = ((), (), s32[]{:S(2)}) async-start(), calls=%async_computation.4 | async-start | bytes 786432 | tf_op jit(solution)/shard_map/reduce_scatter | solution.py:78
  52.6 4.7 %copy-start.6 = (bf16[2,512,512]{2,1,0:T(8,128)(2,1)S(1)}, bf16[2,512,512]{2,1,0:T(8,128)(2,1)}, u32[]{:S(2)}) copy-start(bf16[2,512,512]{2,1,0:T(8,128)(2,1)} %param.15) | copy-start | bytes 3145732
  61.1 21.6 %copy-start.2 = (bf16[256,512]{1,0:T(8,128)(2,1)}, bf16[256,512]{1,0:T(8,128)(2,1)S(1)}, u32[]{:S(2)}) copy-start(bf16[256,512]{1,0:T(8,128)(2,1)S(1)} %get-tuple-element.19) | copy-start | bytes 786436
  61.1 8.3 %collective-permute-start.4 = (bf16[1,1,128,512]{3,2,1,0:T(8,128)(2,1)S(1)}, bf16[1,1,128,512]{3,2,1,0:T(8,128)(2,1)S(1)}, u32[]{:S(2)}, u32[]{:S(2)}) collective-permute-start(bf16[1,1,128,512]{3,2,1,0:T(8,128)(2,1)S(1)} %slice_bitcast_fusion.6), channel_id=1, source_target_pairs={{0,4},{4,8},{8,12},{12,0},{1,5},{5,9},{9,13},{13,1},{2,6},{6,10},{... | collective-permute-start | bytes 393224 | tf_op jit(solution)/shard_map/ppermute | solution.py:14
  62.9 7.6 %collective-permute-start.5 = (bf16[1,1,128,512]{3,2,1,0:T(8,128)(2,1)S(1)}, bf16[1,1,128,512]{3,2,1,0:T(8,128)(2,1)S(1)}, u32[]{:S(2)}, u32[]{:S(2)}) collective-permute-start(bf16[1,1,128,512]{3,2,1,0:T(8,128)(2,1)S(1)} %slice_bitcast_fusion.6), channel_id=1, source_target_pairs={{4,0},{8,4},{12,8},{0,12},{5,1},{9,5},{13,9},{1,13},{6,2},{10,6},{... | collective-permute-start | bytes 393224 | tf_op jit(solution)/shard_map/ppermute | solution.py:17
  70.5 12.1 %collective-permute-start.6 = (bf16[3,1,128,512]{3,2,1,0:T(8,128)(2,1)S(1)}, bf16[3,1,128,512]{3,2,1,0:T(8,128)(2,1)S(1)}, u32[]{:S(2)}, u32[]{:S(2)}) collective-permute-start(bf16[3,1,128,512]{3,2,1,0:T(8,128)(2,1)S(1)} %pad_maximum_fusion.2), channel_id=1, source_target_pairs={{0,2},{2,0},{1,3},{3,1},{4,6},{6,4},{5,7},{7,5},{8,10},{10,8},{9,1... | collective-permute-start | bytes 1179656 | tf_op jit(solution)/shard_map/ppermute | solution.py:14
  72.0 17.5 %collective-permute-start.7 = (bf16[3,1,128,512]{3,2,1,0:T(8,128)(2,1)S(1)}, bf16[3,1,128,512]{3,2,1,0:T(8,128)(2,1)S(1)}, u32[]{:S(2)}, u32[]{:S(2)}) collective-permute-start(bf16[3,1,128,512]{3,2,1,0:T(8,128)(2,1)S(1)} %pad_maximum_fusion.2), channel_id=1, source_target_pairs={{2,0},{0,2},{3,1},{1,3},{6,4},{4,6},{7,5},{5,7},{10,8},{8,10},{11,... | collective-permute-start | bytes 1179656 | tf_op jit(solution)/shard_map/ppermute | solution.py:17
  101.8 70.0 %reduce-scatter.8.cloned.1.call-start = ((), (), s32[]{:S(2)}) async-start(), calls=%async_computation.5 | async-start | bytes 1310720 | tf_op jit(solution)/shard_map/reduce_scatter | solution.py:121
  103.7 5.6 %copy-start.3 = (bf16[256,512]{1,0:T(8,128)(2,1)S(1)}, bf16[256,512]{1,0:T(8,128)(2,1)}, u32[]{:S(2)}) copy-start(bf16[256,512]{1,0:T(8,128)(2,1)} %copy-done.2) | copy-start | bytes 786436
  103.7 5.6 %copy-start.17 = (f32[256]{0:T(256)S(1)}, f32[256]{0:T(256)}, u32[]{:S(2)}) copy-start(f32[256]{0:T(256)} %compare_convert_fusion.1) | copy-start | bytes 3076
  103.7 5.6 %copy-start.19 = (bf16[1,1,256,512]{3,2,1,0:T(8,128)(2,1)S(1)}, bf16[1,1,256,512]{3,2,1,0:T(8,128)(2,1)}, u32[]{:S(2)}) copy-start(bf16[1,1,256,512]{3,2,1,0:T(8,128)(2,1)} %param.11) | copy-start | bytes 786436
  105.2 6.4 %copy-start.7 = (bf16[2,512,512]{2,1,0:T(8,128)(2,1)S(1)}, bf16[2,512,512]{2,1,0:T(8,128)(2,1)}, u32[]{:S(2)}) copy-start(bf16[2,512,512]{2,1,0:T(8,128)(2,1)} %multiply_convert_fusion) | copy-start | bytes 3145732
  111.7 5.3 %copy-start.12 = (bf16[256,512]{1,0:T(8,128)(2,1)}, bf16[256,512]{1,0:T(8,128)(2,1)S(1)}, u32[]{:S(2)}) copy-start(bf16[256,512]{1,0:T(8,128)(2,1)S(1)} %get-tuple-element.13) | copy-start | bytes 786436
  112.0 0.7 copy-start.9
  119.1 3.5 %copy-start.18 = (s32[1,1,12]{2,1,0:T(1,128)S(1)}, s32[1,1,12]{2,1,0:T(1,128)}, u32[]{:S(2)}) copy-start(s32[1,1,12]{2,1,0:T(1,128)} %param.13) | copy-start | bytes 148
  127.3 9.1 %copy-start.1 = (f32[512,512]{1,0:T(8,128)S(1)}, f32[512,512]{1,0:T(8,128)}, u32[]{:S(2)}) copy-start(f32[512,512]{1,0:T(8,128)} %squeeze.39) | copy-start | bytes 3145732
  127.3 9.1 %copy-start.4 = (bf16[256,512]{1,0:T(8,128)(2,1)S(1)}, bf16[256,512]{1,0:T(8,128)(2,1)}, u32[]{:S(2)}) copy-start(bf16[256,512]{1,0:T(8,128)(2,1)} %copy-done.2) | copy-start | bytes 786436
  127.3 9.1 %copy-start.11 = (bf16[256,512]{1,0:T(8,128)(2,1)S(1)}, bf16[256,512]{1,0:T(8,128)(2,1)}, u32[]{:S(2)}) copy-start(bf16[256,512]{1,0:T(8,128)(2,1)} %reduce-scatter.6.cloned.1.call-done) | copy-start | bytes 786436
  127.3 9.0 %copy-start.13 = (bf16[256,512]{1,0:T(8,128)(2,1)S(1)}, bf16[256,512]{1,0:T(8,128)(2,1)}, u32[]{:S(2)}) copy-start(bf16[256,512]{1,0:T(8,128)(2,1)} %copy-done.12) | copy-start | bytes 786436
  127.4 9.4 %collective-permute-start.10 = (bf16[1,128,512]{2,1,0:T(8,128)(2,1)S(1)}, bf16[1,128,512]{2,1,0:T(8,128)(2,1)S(1)}, u32[]{:S(2)}, u32[]{:S(2)}) collective-permute-start(bf16[1,128,512]{2,1,0:T(8,128)(2,1)S(1)} %get-tuple-element.9), channel_id=1, source_target_pairs={{0,2},{1,3},{4,6},{5,7},{8,10},{9,11},{12,14},{13,15},{16,18},{17,... | collective-permute-start | bytes 393224 | tf_op jit(solution)/shard_map/ppermute | solution.py:14
  131.1 7.3 %collective-permute-start.11 = (bf16[1,128,512]{2,1,0:T(8,128)(2,1)S(1)}, bf16[1,128,512]{2,1,0:T(8,128)(2,1)S(1)}, u32[]{:S(2)}, u32[]{:S(2)}) collective-permute-start(bf16[1,128,512]{2,1,0:T(8,128)(2,1)S(1)} %get-tuple-element.8), channel_id=1, source_target_pairs={{2,0},{3,1},{6,4},{7,5},{10,8},{11,9},{14,12},{15,13},{18,16},{19,... | collective-permute-start | bytes 393224 | tf_op jit(solution)/shard_map/ppermute | solution.py:17
  132.4 8.2 %collective-permute-start.8 = (bf16[1,128,512]{2,1,0:T(8,128)(2,1)S(1)}, bf16[1,128,512]{2,1,0:T(8,128)(2,1)S(1)}, u32[]{:S(2)}, u32[]{:S(2)}) collective-permute-start(bf16[1,128,512]{2,1,0:T(8,128)(2,1)S(1)} %get-tuple-element.7), channel_id=1, source_target_pairs={{0,4},{4,8},{8,12},{12,0},{1,5},{5,9},{9,13},{13,1},{2,6},{6,10},{... | collective-permute-start | bytes 393224 | tf_op jit(solution)/shard_map/ppermute | solution.py:14
  134.0 8.0 %collective-permute-start.9 = (bf16[1,128,512]{2,1,0:T(8,128)(2,1)S(1)}, bf16[1,128,512]{2,1,0:T(8,128)(2,1)S(1)}, u32[]{:S(2)}, u32[]{:S(2)}) collective-permute-start(bf16[1,128,512]{2,1,0:T(8,128)(2,1)S(1)} %get-tuple-element.10), channel_id=1, source_target_pairs={{4,0},{8,4},{12,8},{0,12},{5,1},{9,5},{13,9},{1,13},{6,2},{10,6},{... | collective-permute-start | bytes 393224 | tf_op jit(solution)/shard_map/ppermute | solution.py:17
  136.3 5.7 %copy-start.22 = (f32[256,512]{1,0:T(8,128)S(1)}, f32[256,512]{1,0:T(8,128)}, u32[]{:S(2)}) copy-start(f32[256,512]{1,0:T(8,128)} %get-tuple-element.20) | copy-start | bytes 1572868
  136.7 5.4 %copy-start.5 = (f32[512,512]{1,0:T(8,128)S(1)}, f32[512,512]{1,0:T(8,128)}, u32[]{:S(2)}) copy-start(f32[512,512]{1,0:T(8,128)} %squeeze.38) | copy-start | bytes 3145732
  136.7 5.4 %copy-start.8 = (bf16[1,1,256,512]{3,2,1,0:T(8,128)(2,1)S(1)}, bf16[1,1,256,512]{3,2,1,0:T(8,128)(2,1)}, u32[]{:S(2)}) copy-start(bf16[1,1,256,512]{3,2,1,0:T(8,128)(2,1)} %param.10) | copy-start | bytes 786436
  136.7 5.4 %copy-start.10 = (bf16[256,512]{1,0:T(8,128)(2,1)S(1)}, bf16[256,512]{1,0:T(8,128)(2,1)}, u32[]{:S(2)}) copy-start(bf16[256,512]{1,0:T(8,128)(2,1)} %copy-done.9) | copy-start | bytes 786436
  136.7 5.4 %copy-start.20 = (bf16[1,1,256,512]{3,2,1,0:T(8,128)(2,1)S(1)}, bf16[1,1,256,512]{3,2,1,0:T(8,128)(2,1)}, u32[]{:S(2)}) copy-start(bf16[1,1,256,512]{3,2,1,0:T(8,128)(2,1)} %param.11) | copy-start | bytes 786436
  136.7 5.4 %copy-start.21 = (bf16[256,512]{1,0:T(8,128)(2,1)S(1)}, bf16[256,512]{1,0:T(8,128)(2,1)}, u32[]{:S(2)}) copy-start(bf16[256,512]{1,0:T(8,128)(2,1)} %reduce-scatter.4.cloned.1.call-done) | copy-start | bytes 786436
  143.8 47.1 %all-reduce.3.cloned.1.call-start = ((), (), s32[]{:S(2)}) async-start(), calls=%async_computation.6 | async-start | bytes 524288 | tf_op jit(solution)/shard_map/psum | solution.py:122
  171.8 45.7 %all-reduce.5.cloned.1.call-start = ((), (), s32[]{:S(2)}) async-start(), calls=%async_computation.7 | async-start | bytes 524288 | tf_op jit(solution)/shard_map/psum | solution.py:122
Sparse Core Ops, SparseCore 0:
  50.3 7.6 reduce-scatter.3
  101.9 7.3 reduce-scatter.5
  143.9 27.7 reduce-scatter.7
  174.0 16.8 all-reduce.2
  193.1 24.3 all-reduce.4
